TPU v7x, 32 devices: a whole 2x2x4 slice. The times are simulated.
32 devices in a mesh: probe: 2 (over x), space: 16 (over z, y, core).
Axes of the slice: x: 2, y: 2, z: 4, core: 2. Of those that a mesh axis runs over, the one named last changes fastest.
Arguments:
- field_before: float32 [2, 64, 256, 256], P('probe', 'space'), may hold values from -6 to 6
- field_now: float32 [2, 64, 256, 256], P('probe', 'space'), may hold values from -6 to 6
- stiffness: float32 [64, 256, 256], P('space'), may hold values from 0.04 to 0.1
- buoyancy: float32 [64, 256, 256], P('space'), may hold values from 0.6 to 1.4
- perturbation: float32 [2, 64, 256, 256], P('probe', 'space'), may hold values from -0.25 to 0.25
Outputs:
- field_after: float32 [2, 64, 256, 256], P('probe', 'space')
All inputs are finite; a program needn't handle non-finite values.
Results may differ from a plain program's by a relative error of at most 0.00002.
Values sent between devices are 32-bit elements; how exact they have to be, the bound alone decides.
No kernel may reach another device: no remote copies, remote signals or barrier semaphores. Data moves between devices by JAX's collectives and lax.ppermute only.
A program may use at most 128 MiB of HBM per device.

v0:
```python
import jax
import jax.numpy as jnp
from jax import lax
from jax.sharding import PartitionSpec as P

STEPS = 2
second_coeffs = (8.0 / 5.0, -1.0 / 5.0, 8.0 / 315.0, -1.0 / 560.0)
first_coeffs = (4.0 / 5.0, -1.0 / 5.0, 4.0 / 105.0, -1.0 / 280.0)
centre_coeff = -205.0 / 72.0


def with_halo(block, sides, width):
    for axis, dim in sides:
        count = lax.axis_size(axis)
        forward = [(i, i + 1) for i in range(count - 1)]
        backward = [(target, source) for source, target in forward]
        low = lax.ppermute(
            lax.slice_in_dim(block, block.shape[dim] - width, None, axis=dim), axis, forward
        )
        high = lax.ppermute(lax.slice_in_dim(block, 0, width, axis=dim), axis, backward)
        block = jnp.concatenate([low, block, high], axis=dim)
    return block


def spread(block, axis, owner):
    block = jnp.where(lax.axis_index(axis) == owner, block, jnp.zeros_like(block))
    return lax.psum(block, axis)


def shifted(padded, direction, offset):
    window = [
        slice(4, padded.shape[0] - 4),
        slice(4, padded.shape[1] - 4),
        slice(4, padded.shape[2] - 4),
    ]
    window[direction] = slice(4 + offset, padded.shape[direction] - 4 + offset)
    return padded[tuple(window)]


def second_sum(padded):
    total = 3.0 * centre_coeff * shifted(padded, 0, 0)
    for direction in range(3):
        for reach in range(1, 5):
            total = total + second_coeffs[reach - 1] * (
                shifted(padded, direction, reach) + shifted(padded, direction, -reach)
            )
    return total


def first_parts(padded):
    parts = []
    for direction in range(3):
        total = jnp.zeros_like(shifted(padded, 0, 0))
        for reach in range(1, 5):
            total = total + first_coeffs[reach - 1] * (
                shifted(padded, direction, reach) - shifted(padded, direction, -reach)
            )
        parts.append(total)
    return parts


def pad_sides(extended):
    return jnp.pad(extended, ((0, 0), (4, 4), (4, 4)))


def divergence(padded, buoyancy, slope):
    grads = first_parts(padded)
    return (
        buoyancy * second_sum(padded)
        + slope[0] * grads[0]
        + slope[1] * grads[1]
        + slope[2] * grads[2]
    )


def on_device(field_before, field_now, stiffness, buoyancy, perturbation):
    rim = with_halo(buoyancy - 1.0, (("space", 0),), 4)
    slope = first_parts(pad_sides(rim))
    born_flag = (lax.axis_index("probe") > 0).astype(jnp.float32)
    source_scale = born_flag * perturbation[0]

    def operate(extended):
        return divergence(pad_sides(extended), buoyancy, slope)

    before = field_before[0]
    now = field_now[0]
    for step in range(STEPS):
        base = spread(now, "probe", 0)
        both = with_halo(jnp.stack([base, now]), (("space", 1),), 4)
        base_term = operate(both[0])
        own_term = operate(both[1])
        following = 2.0 * now - before + stiffness * own_term + source_scale * base_term
        before, now = (now, following)
    return now[None]


def solution(mesh):
    placed = (
        P("probe", "space", None, None),
        P("probe", "space", None, None),
        P("space", None, None),
        P("space", None, None),
        P("probe", "space", None, None),
    )
    return jax.shard_map(
        on_device,
        mesh=mesh,
        in_specs=placed,
        out_specs=P("probe", "space", None, None),
        check_vma=False,
    )
```

profile of v0, /device:TPU:9, one launch (start us, length us, event | category | flops | bytes accessed | tf_op | source)
XLA Modules:
  0.0 317.0 jit_solution(4905952962133589606)
XLA Ops:
  6.5 0.0 copy-start.4
  6.5 0.0 all-reduce.8.cloned.1.call-start
  6.5 2.4 bitcast_select_fusion
  8.9 0.0 all-reduce.8.cloned.1.call-update
  8.9 0.0 all-reduce.10.cloned.1.call-start
  9.0 41.9 %all-reduce.8.cloned.1.call-done = f32[4,256,256]{2,1,0:T(8,128)} async-done(((f32[4,256,256]{2,1,0:T(8,128)}), f32[4,256,256]{2,1,0:T(8,128)}) %all-reduce.8.cloned.1.call-update) | async-done | bytes 1048592 | tf_op jit(solution)/shard_map/psum | solution.py:27
  50.9 3.0 pad_maximum_fusion.4
  53.9 3.6 %collective-permute-start.1 = (f32[2,4,256,256]{3,2,1,0:T(8,128)}, f32[2,4,256,256]{3,2,1,0:T(8,128)S(1)}, u32[]{:S(2)}, u32[]{:S(2)}) collective-permute-start(f32[2,4,256,256]{3,2,1,0:T(8,128)} %pad_maximum_fusion.4), channel_id=1, source_target_pairs={{0,1},{1,2},{2,3},{3,4},{4,5},{5,6},{6,7},{7,8},{8,9},{9,10},{10,1... | collective-permute-start | bytes 6291464 | tf_op jit(solution)/shard_map/ppermute | solution.py:17
  57.6 1.9 collective-permute-start
  59.5 0.0 copy-done.4
  59.5 1.1 broadcast_add_fusion
  60.6 0.0 copy-start
  60.6 3.8 %collective-permute-start.3 = (f32[4,256,256]{2,1,0:T(8,128)}, f32[4,256,256]{2,1,0:T(8,128)}, u32[]{:S(2)}, u32[]{:S(2)}) collective-permute-start(f32[4,256,256]{2,1,0:T(8,128)} %broadcast_add_fusion), channel_id=1, source_target_pairs={{0,1},{1,2},{2,3},{3,4},{4,5},{5,6},{6,7},{7,8},{8,9},{9,10},{10,1... | collective-permute-start | bytes 3145736 | tf_op jit(solution)/shard_map/ppermute | solution.py:17
  64.3 1.9 collective-permute-start.2
  66.3 0.0 copy-start.2
  66.3 59.5 %collective-permute-done.3 = f32[4,256,256]{2,1,0:T(8,128)} collective-permute-done((f32[4,256,256]{2,1,0:T(8,128)}, f32[4,256,256]{2,1,0:T(8,128)}, u32[]{:S(2)}, u32[]{:S(2)}) %collective-permute-start.3) | collective-permute-done | bytes 1048608 | tf_op jit(solution)/shard_map/ppermute | solution.py:17
  125.8 1.6 collective-permute-done.2
  127.4 5.4 %select_maximum_fusion = f32[12,264,264]{2,1,0:T(8,128)} fusion(f32[4,256,256]{2,1,0:T(8,128)} %collective-permute-done.2, f32[4,256,256]{2,1,0:T(8,128)} %broadcast_add_fusion, f32[4,256,256]{2,1,0:T(8,128)} %collective-permute-done.3), kind=kLoop, calls=%fused_computation.70 | loop fusion | flops 12545280 | bytes 6491136 | tf_op jit(solution)/shard_map/concatenate | solution.py:21
  132.8 0.0 collective-permute-done.1
  132.8 0.0 copy-start.1
  132.8 0.0 collective-permute-done
  132.8 0.0 copy-done
  132.8 0.0 copy-done.2
  132.8 2.7 pad_maximum_fusion
  135.5 3.2 %slice_bitcast_fusion.3 = (f32[12,256,256]{2,1,0:T(8,128)}, f32[12,256,256]{2,1,0:T(8,128)}) fusion(f32[2,12,256,256]{3,2,1,0:T(8,128)S(1)} %pad_maximum_fusion), kind=kLoop, calls=%fused_computation.82 | loop fusion | bytes 12582912 | tf_op jit(solution)/shard_map/squeeze | solution.py:91
  138.8 0.0 copy-done.1
  138.8 5.0 %pad_maximum_fusion.2 = (f32[2,8,256,256]{3,2,1,0:T(8,128)}, f32[2,8,256,256]{3,2,1,0:T(8,128)}) fusion(f32[2,4,256,256]{3,2,1,0:T(8,128)} %collective-permute-done, f32[1,4,256,256]{3,2,1,0:T(8,128)S(1)} %copy-done, f32[1,4,256,256]{3,2,1,0:T(8,128)S(1)} %bitcast.239, f32[2,4,256,256]{3,2,1,0:T(8,128)S(1)} %collective-permute-done.1), kind=kLoop, calls=%fused_computation.75 | loop fusion | flops 4194304 | bytes 14680064 | tf_op jit(solution)/shard_map/concatenate | solution.py:21
  143.8 45.2 %broadcast_select_fusion = (f32[4,256,256]{2,1,0:T(8,128)}, f32[4,256,256]{2,1,0:T(8,128)S(1)}, f32[4,256,256]{2,1,0:T(8,128)}, f32[4,256,256]{2,1,0:T(8,128)}, f32[4,256,256]{2,1,0:T(8,128)}) fusion(pred[]{:T(512)S(6)} %eq.4, f32[4,256,256]{2,1,0:T(8,128)} %param.8, f32[12,256,256]{2,1,0:T(8,128)} %get-tuple-element.13, f32[2,4,256,256]{3,2,1,0:T(8,128)} %copy-done.1, ...), kind=kLoop, calls=%fused_computation.213 | loop fusion | flops 52690944 | bytes 54525956 | tf_op jit(solution)/shard_map/jit(_where)/select_n | solution.py:26
  189.0 0.0 all-reduce.10.cloned.1.call-update
  189.0 38.8 %all-reduce.10.cloned.1.call-done = f32[4,256,256]{2,1,0:T(8,128)} async-done(((f32[4,256,256]{2,1,0:T(8,128)}), f32[4,256,256]{2,1,0:T(8,128)}) %all-reduce.10.cloned.1.call-update) | async-done | bytes 1048592 | tf_op jit(solution)/shard_map/psum | solution.py:27
  227.8 0.0 copy-start.3
  227.8 1.4 pad_maximum_fusion.5
  229.2 3.7 %collective-permute-start.5 = (f32[2,4,256,256]{3,2,1,0:T(8,128)S(1)}, f32[2,4,256,256]{3,2,1,0:T(8,128)S(1)}, u32[]{:S(2)}, u32[]{:S(2)}) collective-permute-start(f32[2,4,256,256]{3,2,1,0:T(8,128)S(1)} %pad_maximum_fusion.5), channel_id=1, source_target_pairs={{0,1},{1,2},{2,3},{3,4},{4,5},{5,6},{6,7},{7,8},{8,9},{9,10},{10,1... | collective-permute-start | bytes 6291464 | tf_op jit(solution)/shard_map/ppermute | solution.py:17
  232.9 2.1 collective-permute-start.4
  235.0 43.3 %collective-permute-done.5 = f32[2,4,256,256]{3,2,1,0:T(8,128)S(1)} collective-permute-done((f32[2,4,256,256]{3,2,1,0:T(8,128)S(1)}, f32[2,4,256,256]{3,2,1,0:T(8,128)S(1)}, u32[]{:S(2)}, u32[]{:S(2)}) %collective-permute-start.5) | collective-permute-done | bytes 2097184 | tf_op jit(solution)/shard_map/ppermute | solution.py:17
  278.3 1.6 collective-permute-done.4
  279.9 0.0 copy-done.3
  279.9 0.5 pad_maximum_fusion.1
  280.4 3.3 %slice_bitcast_fusion.1 = (f32[12,256,256]{2,1,0:T(8,128)}, f32[12,256,256]{2,1,0:T(8,128)}) fusion(f32[2,12,256,256]{3,2,1,0:T(8,128)S(1)} %pad_maximum_fusion.1), kind=kLoop, calls=%fused_computation.80 | loop fusion | bytes 12582912 | tf_op jit(solution)/shard_map/squeeze | solution.py:91
  283.7 0.0 copy-start.5
  283.7 0.9 pad_maximum_fusion.3
  284.6 0.3 copy-done.5
  284.9 25.3 %fusion.35 = f32[1,4,256,256]{3,2,1,0:T(8,128)} fusion(f32[4,256,256]{2,1,0:T(8,128)} %get-tuple-element.9, f32[4,256,256]{2,1,0:T(8,128)S(1)} %copy-done.5, f32[4,256,256]{2,1,0:T(8,128)} %param.7, f32[1,4,256,256]{3,2,1,0:T(8,128)S(1)} %copy-done, f32[4,256,256]{2,1,0:T(8,128)} %get-tuple-element.8, f32[4,256,256]{2,1,0:T(8,128)} %get-tuple-element.7, ...), kind=kLoop, calls=%fused_computation.136 | loop fusion | flops 42205184 | bytes 33554436 | tf_op jit(solution)/shard_map/broadcast_in_dim | solution.py:94
Async XLA Ops:
  6.5 53.0 %copy-start.4 = (f32[4,256,256]{2,1,0:T(8,128)S(1)}, f32[4,256,256]{2,1,0:T(8,128)}, u32[]{:S(2)}) copy-start(f32[4,256,256]{2,1,0:T(8,128)} %param.8) | copy-start | bytes 3145732
  6.5 44.4 %all-reduce.8.cloned.1.call-start = ((), (), s32[]{:S(2)}) async-start(), calls=%async_computation | async-start | bytes 2097152 | tf_op jit(solution)/shard_map/psum | solution.py:27
  8.9 218.8 %all-reduce.10.cloned.1.call-start = ((), (), s32[]{:S(2)}) async-start(), calls=%async_computation.1 | async-start | bytes 2097152 | tf_op jit(solution)/shard_map/psum | solution.py:27
  53.9 78.8 %collective-permute-start.1 = (f32[2,4,256,256]{3,2,1,0:T(8,128)}, f32[2,4,256,256]{3,2,1,0:T(8,128)S(1)}, u32[]{:S(2)}, u32[]{:S(2)}) collective-permute-start(f32[2,4,256,256]{3,2,1,0:T(8,128)} %pad_maximum_fusion.4), channel_id=1, source_target_pairs={{0,1},{1,2},{2,3},{3,4},{4,5},{5,6},{6,7},{7,8},{8,9},{9,10},{10,1... | collective-permute-start | bytes 6291464 | tf_op jit(solution)/shard_map/ppermute | solution.py:17
  57.6 75.2 %collective-permute-start = (f32[2,4,256,256]{3,2,1,0:T(8,128)}, f32[2,4,256,256]{3,2,1,0:T(8,128)}, u32[]{:S(2)}, u32[]{:S(2)}) collective-permute-start(f32[2,4,256,256]{3,2,1,0:T(8,128)} %pad_maximum_fusion.4), channel_id=1, source_target_pairs={{1,0},{2,1},{3,2},{4,3},{5,4},{6,5},{7,6},{8,7},{9,8},{10,9},{11,1... | collective-permute-start | bytes 6291464 | tf_op jit(solution)/shard_map/ppermute | solution.py:20
  60.6 72.2 %copy-start = (f32[1,4,256,256]{3,2,1,0:T(8,128)S(1)}, f32[1,4,256,256]{3,2,1,0:T(8,128)}, u32[]{:S(2)}) copy-start(f32[1,4,256,256]{3,2,1,0:T(8,128)} %param.6) | copy-start | bytes 3145732
  60.6 65.2 %collective-permute-start.3 = (f32[4,256,256]{2,1,0:T(8,128)}, f32[4,256,256]{2,1,0:T(8,128)}, u32[]{:S(2)}, u32[]{:S(2)}) collective-permute-start(f32[4,256,256]{2,1,0:T(8,128)} %broadcast_add_fusion), channel_id=1, source_target_pairs={{0,1},{1,2},{2,3},{3,4},{4,5},{5,6},{6,7},{7,8},{8,9},{9,10},{10,1... | collective-permute-start | bytes 3145736 | tf_op jit(solution)/shard_map/ppermute | solution.py:17
  64.3 63.1 %collective-permute-start.2 = (f32[4,256,256]{2,1,0:T(8,128)}, f32[4,256,256]{2,1,0:T(8,128)}, u32[]{:S(2)}, u32[]{:S(2)}) collective-permute-start(f32[4,256,256]{2,1,0:T(8,128)} %broadcast_add_fusion), channel_id=1, source_target_pairs={{1,0},{2,1},{3,2},{4,3},{5,4},{6,5},{7,6},{8,7},{9,8},{10,9},{11,1... | collective-permute-start | bytes 3145736 | tf_op jit(solution)/shard_map/ppermute | solution.py:20
  66.3 66.5 %copy-start.2 = (f32[4,256,256]{2,1,0:T(8,128)S(1)}, f32[4,256,256]{2,1,0:T(8,128)}, u32[]{:S(2)}) copy-start(f32[4,256,256]{2,1,0:T(8,128)} %all-reduce.8.cloned.1.call-done) | copy-start | bytes 3145732
  132.8 6.0 %copy-start.1 = (f32[2,4,256,256]{3,2,1,0:T(8,128)}, f32[2,4,256,256]{3,2,1,0:T(8,128)S(1)}, u32[]{:S(2)}) copy-start(f32[2,4,256,256]{3,2,1,0:T(8,128)S(1)} %collective-permute-done.1) | copy-start | bytes 6291460
  227.8 52.2 %copy-start.3 = (f32[4,256,256]{2,1,0:T(8,128)S(1)}, f32[4,256,256]{2,1,0:T(8,128)}, u32[]{:S(2)}) copy-start(f32[4,256,256]{2,1,0:T(8,128)} %all-reduce.10.cloned.1.call-done) | copy-start | bytes 3145732
  229.2 49.1 %collective-permute-start.5 = (f32[2,4,256,256]{3,2,1,0:T(8,128)S(1)}, f32[2,4,256,256]{3,2,1,0:T(8,128)S(1)}, u32[]{:S(2)}, u32[]{:S(2)}) collective-permute-start(f32[2,4,256,256]{3,2,1,0:T(8,128)S(1)} %pad_maximum_fusion.5), channel_id=1, source_target_pairs={{0,1},{1,2},{2,3},{3,4},{4,5},{5,6},{6,7},{7,8},{8,9},{9,10},{10,1... | collective-permute-start | bytes 6291464 | tf_op jit(solution)/shard_map/ppermute | solution.py:17
  232.9 47.0 %collective-permute-start.4 = (f32[2,4,256,256]{3,2,1,0:T(8,128)S(1)}, f32[2,4,256,256]{3,2,1,0:T(8,128)S(1)}, u32[]{:S(2)}, u32[]{:S(2)}) collective-permute-start(f32[2,4,256,256]{3,2,1,0:T(8,128)S(1)} %pad_maximum_fusion.5), channel_id=1, source_target_pairs={{1,0},{2,1},{3,2},{4,3},{5,4},{6,5},{7,6},{8,7},{9,8},{10,9},{11,1... | collective-permute-start | bytes 6291464 | tf_op jit(solution)/shard_map/ppermute | solution.py:20
  283.7 1.2 copy-start.5
Sparse Core Ops, SparseCore 0:
  9.6 41.1 all-reduce.7
  189.1 38.5 all-reduce.9
where the time goes:
time: 317 us
  waiting for transfers between devices  187 us (59%)
  other arithmetic  92.8 us (29%)
  starting transfers between devices  17.1 us (5%)
  between operations  13.5 us (4%)
  local copies, waits for them, and re-layouts  6.93 us (2%)
    ppermute x3, waiting for transfers between devices, with_halo(): lax.ppermute(lax.slice_in_dim(block, block.shape[dim] - width, None, axis...  103 us
    psum x2, waiting for transfers between devices, spread(): return lax.psum(block, axis)  80.7 us
    select_n x2, other arithmetic, spread(): jnp.where(lax.axis_index(axis) == owner, block, jnp.zeros_like(block))  47.6 us
    broadcast_in_dim x1, other arithmetic, on_device(): return now[None]  25.3 us
    concatenate x5, other arithmetic, with_halo(): block = jnp.concatenate([low, block, high], axis=dim)  14.4 us
    ppermute x3, starting transfers between devices, with_halo(): lax.ppermute(lax.slice_in_dim(block, block.shape[dim] - width, None, axis...  11.1 us
    squeeze x2, local copies, waits for them, and re-layouts, on_device(): own_term = operate(both[1])  6.56 us
  transfers between devices with their start and end apart: 8, of which 6 were waited for; matrix products, arithmetic and copies ran while one was open for 2% of the time, Pallas kernels for 0%

commit v1 on v0

--- a/solution.py
+++ b/solution.py
@@ -24,7 +24,7 @@
 
 def spread(block, axis, owner):
     block = jnp.where(lax.axis_index(axis) == owner, block, jnp.zeros_like(block))
-    return lax.psum(block, axis)
+    return jnp.sum(lax.all_gather(block, axis), axis=0)
 
 
 def shifted(padded, direction, offset):

time: 317 us -> 302 us (0.953)
  waiting for transfers between devices: 187 us -> 172 us
    psum x2 -> x0, waiting for transfers between devices: 80.7 us -> none  [spread(): return lax.psum(block, axis)]
    all_gather x0 -> x2, waiting for transfers between devices: none -> 66.1 us  [spread(): return jnp.sum(lax.all_gather(block, axis), axis=0)]
    reduce_sum x0 -> x2, other arithmetic: none -> 3.71 us  [spread(): return jnp.sum(lax.all_gather(block, axis), axis=0)]
where the time goes in v1:
time: 302 us; the launch traced here: 301 us
  waiting for transfers between devices  172 us (57%)
  other arithmetic  91.9 us (30%)
  starting transfers between devices  16.9 us (6%)
  between operations  13.5 us (4%)
  local copies, waits for them, and re-layouts  6.76 us (2%)
    ppermute x3, waiting for transfers between devices, with_halo(): lax.ppermute(lax.slice_in_dim(block, block.shape[dim] - width, None, axis...  103 us
    all_gather x2, waiting for transfers between devices, spread(): return jnp.sum(lax.all_gather(block, axis), axis=0)  66.1 us
    select_n x2, other arithmetic, spread(): jnp.where(lax.axis_index(axis) == owner, block, jnp.zeros_like(block))  46.8 us
    broadcast_in_dim x1, other arithmetic, on_device(): return now[None]  24.3 us
    concatenate x5, other arithmetic, with_halo(): block = jnp.concatenate([low, block, high], axis=dim)  14.3 us
    ppermute x3, starting transfers between devices, with_halo(): lax.ppermute(lax.slice_in_dim(block, block.shape[dim] - width, None, axis...  10.9 us
    squeeze x2, local copies, waits for them, and re-layouts, on_device(): own_term = operate(both[1])  6.32 us
  transfers between devices with their start and end apart: 8, of which 6 were waited for; matrix products, arithmetic and copies ran while one was open for 2% of the time, Pallas kernels for 0%

profile of v1, /device:TPU:9, one launch (start us, length us, event | category | flops | bytes accessed | tf_op | source)
XLA Modules:
  0.0 301.4 jit_solution(5975419288900840642)
XLA Ops:
  6.5 0.0 copy-start
  6.5 0.0 all-gather.4.cloned.1.call-start
  6.5 2.4 broadcast_select_fusion.1
  8.9 0.0 copy-start.1
  8.9 0.0 all-gather.4.cloned.1.call-update
  8.9 0.0 all-gather.6.cloned.1.call-start
  9.0 34.2 %all-gather.4.cloned.1.call-done = f32[2,4,256,256]{3,2,1,0:T(8,128)} async-done(((f32[1,4,256,256]{3,2,1,0:T(8,128)}), f32[2,4,256,256]{3,2,1,0:T(8,128)}) %all-gather.4.cloned.1.call-update) | async-done | bytes 2097168 | tf_op jit(solution)/shard_map/all_gather | solution.py:27
  43.2 1.9 reduce_sum.18
  45.1 0.0 copy-done
  45.1 1.5 pad_maximum_fusion.4
  46.6 3.7 %collective-permute-start.1 = (f32[2,4,256,256]{3,2,1,0:T(8,128)}, f32[2,4,256,256]{3,2,1,0:T(8,128)}, u32[]{:S(2)}, u32[]{:S(2)}) collective-permute-start(f32[2,4,256,256]{3,2,1,0:T(8,128)} %pad_maximum_fusion.4), channel_id=1, source_target_pairs={{0,1},{1,2},{2,3},{3,4},{4,5},{5,6},{6,7},{7,8},{8,9},{9,10},{10,1... | collective-permute-start | bytes 6291464 | tf_op jit(solution)/shard_map/ppermute | solution.py:17
  50.3 1.9 collective-permute-start
  52.2 0.0 copy-done.1
  52.2 1.1 broadcast_add_fusion
  53.3 3.6 %collective-permute-start.3 = (f32[4,256,256]{2,1,0:T(8,128)}, f32[4,256,256]{2,1,0:T(8,128)S(1)}, u32[]{:S(2)}, u32[]{:S(2)}) collective-permute-start(f32[4,256,256]{2,1,0:T(8,128)} %broadcast_add_fusion), channel_id=1, source_target_pairs={{0,1},{1,2},{2,3},{3,4},{4,5},{5,6},{6,7},{7,8},{8,9},{9,10},{10,1... | collective-permute-start | bytes 3145736 | tf_op jit(solution)/shard_map/ppermute | solution.py:17
  56.9 1.9 collective-permute-start.2
  58.9 59.6 %collective-permute-done.3 = f32[4,256,256]{2,1,0:T(8,128)S(1)} collective-permute-done((f32[4,256,256]{2,1,0:T(8,128)}, f32[4,256,256]{2,1,0:T(8,128)S(1)}, u32[]{:S(2)}, u32[]{:S(2)}) %collective-permute-start.3) | collective-permute-done | bytes 1048608 | tf_op jit(solution)/shard_map/ppermute | solution.py:17
  118.5 0.0 copy-start.3
  118.5 1.6 collective-permute-done.2
  120.1 5.2 %select_maximum_fusion = f32[12,264,264]{2,1,0:T(8,128)} fusion(f32[4,256,256]{2,1,0:T(8,128)} %collective-permute-done.2, f32[4,256,256]{2,1,0:T(8,128)} %broadcast_add_fusion, f32[4,256,256]{2,1,0:T(8,128)S(1)} %collective-permute-done.3), kind=kLoop, calls=%fused_computation.70 | loop fusion | flops 12545280 | bytes 6491136 | tf_op jit(solution)/shard_map/concatenate | solution.py:21
  125.3 0.0 collective-permute-done.1
  125.4 0.0 collective-permute-done
  125.4 2.5 pad_maximum_fusion
  127.9 0.0 copy-done.3
  127.9 3.3 %slice_bitcast_fusion.3 = (f32[12,256,256]{2,1,0:T(8,128)}, f32[12,256,256]{2,1,0:T(8,128)}) fusion(f32[2,12,256,256]{3,2,1,0:T(8,128)S(1)} %pad_maximum_fusion), kind=kLoop, calls=%fused_computation.82 | loop fusion | bytes 12582912 | tf_op jit(solution)/shard_map/squeeze | solution.py:91
  131.1 5.2 %pad_maximum_fusion.2 = (f32[2,8,256,256]{3,2,1,0:T(8,128)}, f32[2,8,256,256]{3,2,1,0:T(8,128)}) fusion(f32[2,4,256,256]{3,2,1,0:T(8,128)} %collective-permute-done, f32[1,4,256,256]{3,2,1,0:T(8,128)S(1)} %copy-done, f32[1,4,256,256]{3,2,1,0:T(8,128)S(1)} %bitcast.239, f32[2,4,256,256]{3,2,1,0:T(8,128)} %collective-permute-done.1), kind=kLoop, calls=%fused_computation.75 | loop fusion | flops 4194304 | bytes 14680064 | tf_op jit(solution)/shard_map/concatenate | solution.py:21
  136.4 44.4 %broadcast_select_fusion = (f32[4,256,256]{2,1,0:T(8,128)}, f32[4,256,256]{2,1,0:T(8,128)S(1)}, f32[4,256,256]{2,1,0:T(8,128)}, f32[4,256,256]{2,1,0:T(8,128)}, f32[4,256,256]{2,1,0:T(8,128)}) fusion(pred[]{:T(512)S(6)} %eq.4, f32[4,256,256]{2,1,0:T(8,128)} %param.8, f32[12,256,256]{2,1,0:T(8,128)} %get-tuple-element.13, ...), kind=kLoop, calls=%fused_computation.211 | loop fusion | flops 52690944 | bytes 54525956 | tf_op jit(solution)/shard_map/jit(_where)/select_n | solution.py:26
  180.8 0.0 all-gather.6.cloned.1.call-update
  180.9 31.8 %all-gather.6.cloned.1.call-done = f32[8,256,256]{2,1,0:T(8,128)} async-done(((f32[4,256,256]{2,1,0:T(8,128)}), f32[8,256,256]{2,1,0:T(8,128)}) %all-gather.6.cloned.1.call-update) | async-done | bytes 2097168 | tf_op jit(solution)/shard_map/all_gather | solution.py:27
  212.7 1.9 reduce_sum.19
  214.6 0.1 pad_maximum_fusion.5
  214.7 3.7 %collective-permute-start.5 = (f32[2,4,256,256]{3,2,1,0:T(8,128)S(1)}, f32[2,4,256,256]{3,2,1,0:T(8,128)S(1)}, u32[]{:S(2)}, u32[]{:S(2)}) collective-permute-start(f32[2,4,256,256]{3,2,1,0:T(8,128)S(1)} %pad_maximum_fusion.5), channel_id=1, source_target_pairs={{0,1},{1,2},{2,3},{3,4},{4,5},{5,6},{6,7},{7,8},{8,9},{9,10},{10,1... | collective-permute-start | bytes 6291464 | tf_op jit(solution)/shard_map/ppermute | solution.py:17
  218.4 2.1 collective-permute-start.4
  220.5 43.3 %collective-permute-done.5 = f32[2,4,256,256]{3,2,1,0:T(8,128)S(1)} collective-permute-done((f32[2,4,256,256]{3,2,1,0:T(8,128)S(1)}, f32[2,4,256,256]{3,2,1,0:T(8,128)S(1)}, u32[]{:S(2)}, u32[]{:S(2)}) %collective-permute-start.5) | collective-permute-done | bytes 2097184 | tf_op jit(solution)/shard_map/ppermute | solution.py:17
  263.8 1.6 collective-permute-done.4
  265.4 0.5 pad_maximum_fusion.1
  266.0 3.1 %slice_bitcast_fusion.1 = (f32[12,256,256]{2,1,0:T(8,128)}, f32[12,256,256]{2,1,0:T(8,128)}) fusion(f32[2,12,256,256]{3,2,1,0:T(8,128)S(1)} %pad_maximum_fusion.1), kind=kLoop, calls=%fused_computation.80 | loop fusion | bytes 12582912 | tf_op jit(solution)/shard_map/squeeze | solution.py:91
  269.1 0.0 copy-start.2
  269.1 0.8 pad_maximum_fusion.3
  269.8 0.4 copy-done.2
  270.3 24.3 %fusion.35 = f32[1,4,256,256]{3,2,1,0:T(8,128)} fusion(f32[4,256,256]{2,1,0:T(8,128)} %get-tuple-element.9, f32[4,256,256]{2,1,0:T(8,128)S(1)} %copy-done.2, f32[4,256,256]{2,1,0:T(8,128)} %param.7, f32[1,4,256,256]{3,2,1,0:T(8,128)S(1)} %copy-done, f32[4,256,256]{2,1,0:T(8,128)} %get-tuple-element.8, f32[4,256,256]{2,1,0:T(8,128)} %get-tuple-element.7, ...), kind=kLoop, calls=%fused_computation.136 | loop fusion | flops 42205184 | bytes 33554436 | tf_op jit(solution)/shard_map/broadcast_in_dim | solution.py:94
Async XLA Ops:
  6.5 38.5 %copy-start = (f32[1,4,256,256]{3,2,1,0:T(8,128)S(1)}, f32[1,4,256,256]{3,2,1,0:T(8,128)}, u32[]{:S(2)}) copy-start(f32[1,4,256,256]{3,2,1,0:T(8,128)} %param.6) | copy-start | bytes 3145732
  6.5 36.7 %all-gather.4.cloned.1.call-start = ((), (), s32[]{:S(2)}) async-start(), calls=%async_computation | async-start | bytes 3145728 | tf_op jit(solution)/shard_map/all_gather | solution.py:27
  8.9 43.3 %copy-start.1 = (f32[4,256,256]{2,1,0:T(8,128)S(1)}, f32[4,256,256]{2,1,0:T(8,128)}, u32[]{:S(2)}) copy-start(f32[4,256,256]{2,1,0:T(8,128)} %param.8) | copy-start | bytes 3145732
  8.9 203.8 %all-gather.6.cloned.1.call-start = ((), (), s32[]{:S(2)}) async-start(), calls=%async_computation.1 | async-start | bytes 3145728 | tf_op jit(solution)/shard_map/all_gather | solution.py:27
  46.6 78.7 %collective-permute-start.1 = (f32[2,4,256,256]{3,2,1,0:T(8,128)}, f32[2,4,256,256]{3,2,1,0:T(8,128)}, u32[]{:S(2)}, u32[]{:S(2)}) collective-permute-start(f32[2,4,256,256]{3,2,1,0:T(8,128)} %pad_maximum_fusion.4), channel_id=1, source_target_pairs={{0,1},{1,2},{2,3},{3,4},{4,5},{5,6},{6,7},{7,8},{8,9},{9,10},{10,1... | collective-permute-start | bytes 6291464 | tf_op jit(solution)/shard_map/ppermute | solution.py:17
  50.3 75.1 %collective-permute-start = (f32[2,4,256,256]{3,2,1,0:T(8,128)}, f32[2,4,256,256]{3,2,1,0:T(8,128)}, u32[]{:S(2)}, u32[]{:S(2)}) collective-permute-start(f32[2,4,256,256]{3,2,1,0:T(8,128)} %pad_maximum_fusion.4), channel_id=1, source_target_pairs={{1,0},{2,1},{3,2},{4,3},{5,4},{6,5},{7,6},{8,7},{9,8},{10,9},{11,1... | collective-permute-start | bytes 6291464 | tf_op jit(solution)/shard_map/ppermute | solution.py:20
  53.3 65.2 %collective-permute-start.3 = (f32[4,256,256]{2,1,0:T(8,128)}, f32[4,256,256]{2,1,0:T(8,128)S(1)}, u32[]{:S(2)}, u32[]{:S(2)}) collective-permute-start(f32[4,256,256]{2,1,0:T(8,128)} %broadcast_add_fusion), channel_id=1, source_target_pairs={{0,1},{1,2},{2,3},{3,4},{4,5},{5,6},{6,7},{7,8},{8,9},{9,10},{10,1... | collective-permute-start | bytes 3145736 | tf_op jit(solution)/shard_map/ppermute | solution.py:17
  56.9 63.2 %collective-permute-start.2 = (f32[4,256,256]{2,1,0:T(8,128)}, f32[4,256,256]{2,1,0:T(8,128)}, u32[]{:S(2)}, u32[]{:S(2)}) collective-permute-start(f32[4,256,256]{2,1,0:T(8,128)} %broadcast_add_fusion), channel_id=1, source_target_pairs={{1,0},{2,1},{3,2},{4,3},{5,4},{6,5},{7,6},{8,7},{9,8},{10,9},{11,1... | collective-permute-start | bytes 3145736 | tf_op jit(solution)/shard_map/ppermute | solution.py:20
  118.5 9.4 %copy-start.3 = (f32[4,256,256]{2,1,0:T(8,128)}, f32[4,256,256]{2,1,0:T(8,128)S(1)}, u32[]{:S(2)}) copy-start(f32[4,256,256]{2,1,0:T(8,128)S(1)} %collective-permute-done.3) | copy-start | bytes 3145732
  214.7 49.1 %collective-permute-start.5 = (f32[2,4,256,256]{3,2,1,0:T(8,128)S(1)}, f32[2,4,256,256]{3,2,1,0:T(8,128)S(1)}, u32[]{:S(2)}, u32[]{:S(2)}) collective-permute-start(f32[2,4,256,256]{3,2,1,0:T(8,128)S(1)} %pad_maximum_fusion.5), channel_id=1, source_target_pairs={{0,1},{1,2},{2,3},{3,4},{4,5},{5,6},{6,7},{7,8},{8,9},{9,10},{10,1... | collective-permute-start | bytes 6291464 | tf_op jit(solution)/shard_map/ppermute | solution.py:17
  218.4 47.0 %collective-permute-start.4 = (f32[2,4,256,256]{3,2,1,0:T(8,128)S(1)}, f32[2,4,256,256]{3,2,1,0:T(8,128)S(1)}, u32[]{:S(2)}, u32[]{:S(2)}) collective-permute-start(f32[2,4,256,256]{3,2,1,0:T(8,128)S(1)} %pad_maximum_fusion.5), channel_id=1, source_target_pairs={{1,0},{2,1},{3,2},{4,3},{5,4},{6,5},{7,6},{8,7},{9,8},{10,9},{11,1... | collective-permute-start | bytes 6291464 | tf_op jit(solution)/shard_map/ppermute | solution.py:20
  269.1 1.2 copy-start.2
Sparse Core Ops, SparseCore 0:
  9.1 34.1 all-gather.3
  181.0 31.6 all-gather.5
